TPU v7x, 1024 devices: a whole 4x4x32 slice. The times are simulated.
1024 devices in a mesh: dp: 8 (over z_hi, core), fsdp: 128 (over x, z_lo, y).
Axes of the slice: x: 4, y: 4, z: 32 (z_hi: 4, z_lo: 8; z = z_hi * 8 + z_lo), core: 2. Of those that a mesh axis runs over, the one named last changes fastest.
Arguments:
- attention_input: bfloat16 [8192, 1536], P('fsdp', 'dp')
- feedforward_input: bfloat16 [14336, 1536], P('fsdp', 'dp')
- attention_cotangent: bfloat16 [8192, 1536], P(('dp', 'fsdp'))
- feedforward_cotangent: bfloat16 [8192, 1536], P(('dp', 'fsdp'))
- lengths: int32 [24], replicated, may hold values from 16 to 64, as said below
- groups: int32 [24], replicated, may hold values from 0 to 3, as said below
- attention_weight: bfloat16 [8192, 8192], P('fsdp', 'dp'), may hold values from -0.29882812 to 0.29882812
- attention_moment: bfloat16 [8192, 8192], P('fsdp', 'dp'), may hold values from -0.59765625 to 0.59765625
- attention_second: bfloat16 [8192, 8192], P('fsdp', 'dp'), may hold values from 0.0099487305 to 1
- feedforward_weight: bfloat16 [14336, 8192], P('fsdp', 'dp'), may hold values from -0.29882812 to 0.29882812
- feedforward_moment: bfloat16 [14336, 8192], P('fsdp', 'dp'), may hold values from -0.59765625 to 0.59765625
- feedforward_second: bfloat16 [14336, 8192], P('fsdp', 'dp'), may hold values from 0.0099487305 to 1
Outputs:
- new_attention_weight: bfloat16 [8192, 8192], P('fsdp', 'dp')
- new_attention_moment: bfloat16 [8192, 8192], P('fsdp', 'dp')
- new_attention_second: bfloat16 [8192, 8192], P('fsdp', 'dp')
- new_feedforward_weight: bfloat16 [14336, 8192], P('fsdp', 'dp')
- new_feedforward_moment: bfloat16 [14336, 8192], P('fsdp', 'dp')
- new_feedforward_second: bfloat16 [14336, 8192], P('fsdp', 'dp')
Inputs may be any that keep to these rules, and one draw needn't show every extreme that they name: `lengths`: some example has exactly 64 live tokens. `groups`: every group has at least one example.
All inputs are finite; a program needn't handle non-finite values.
Results may differ from a plain program's by a relative error of at most 0.0038.
Values may be sent and summed in bfloat16 or wider, within the bound.
No kernel may reach another device: no remote copies, remote signals or barrier semaphores. Data moves between devices by JAX's collectives and lax.ppermute only.
A program may use at most 64 MiB of HBM per device.

v0:
```python
import jax
import jax.numpy as jnp
from jax import lax
from jax.sharding import Mesh
from jax.sharding import PartitionSpec as P

DP = ("dp_0", "dp_1")
FSDP = ("fsdp_0", "fsdp_1", "fsdp_2")
DP_FSDP = ("dp_0", "dp_1", "fsdp_0", "fsdp_1", "fsdp_2")


first_decay = 0.9
second_decay = 0.95
first_bias = 1.0 - 0.9**10
second_bias = 1.0 - 0.95**10
learn_rate = 0.01
weight_decay = 0.1
epsilon = 1e-08
norm_epsilon = 1e-06


def rows_first(arrays, axis, dims):
    turned = [jnp.moveaxis(a, dim, 0) for a, dim in zip(arrays, dims)]
    both = jnp.concatenate([t.reshape(len(t), -1) for t in turned], axis=1)
    filled, at, done = (lax.all_gather(both, axis, axis=0, tiled=True), 0, [])
    for t, dim in zip(turned, dims):
        share = filled[:, at : at + t[0].size].reshape(-1, *t.shape[1:])
        done.append(jnp.moveaxis(share, 0, dim))
        at += t[0].size
    return tuple(done)


def side_by_side(arrays, axis, dim, along):
    widths = [a.shape[along] for a in arrays]
    both = jnp.concatenate(arrays, axis=along)
    filled = lax.all_gather(both, axis, axis=dim, tiled=True)
    return tuple(jnp.split(filled, [sum(widths[:k]) for k in range(1, len(widths))], axis=along))


def by_axis(shard, axes):
    for axis in axes:
        shard = lax.psum(shard, axis)
    return shard


def live_tokens(lengths, slot_len):
    position = lax.broadcasted_iota(jnp.int32, (lengths.shape[0], slot_len), 1)
    return (position < lengths[:, None]).reshape(-1)


def example_norms(inputs, cotangents, second, slot_len):
    precond = 1.0 / (jnp.sqrt(second.astype(jnp.float32)) + epsilon)
    example_count = inputs.shape[1] // slot_len

    def one_example(example, norm_vals):
        inputs_slot = lax.dynamic_slice_in_dim(inputs, example * slot_len, slot_len, 1)
        grads_slot = lax.dynamic_slice_in_dim(cotangents, example * slot_len, slot_len, 1)
        tile_block = lax.dot_general(
            inputs_slot, grads_slot, (((1,), (1,)), ((), ())), preferred_element_type=jnp.float32
        )
        return norm_vals.at[example].set(jnp.sum(tile_block * tile_block * precond))

    return lax.fori_loop(0, example_count, one_example, jnp.zeros((example_count,), jnp.float32))


def importance(norm_vals, groups):
    strength = jnp.sqrt(norm_vals + norm_epsilon)
    same_group = (groups[:, None] == groups[None, :]).astype(jnp.float32)
    group_total = jnp.sum(same_group * strength[None, :], axis=1)
    group_count = jnp.sum(same_group, axis=1)
    return group_count * strength / group_total


def weighted_gradient(inputs, cotangents, token_weight, example_count):
    scaled = (inputs.astype(jnp.float32) * token_weight[None, :]).astype(jnp.bfloat16)
    product = lax.dot_general(
        scaled, cotangents, (((1,), (1,)), ((), ())), preferred_element_type=jnp.float32
    )
    return product / example_count


def adamw_step(weight, moment, second, gradient):
    moment_new = first_decay * moment.astype(jnp.float32) + (1.0 - first_decay) * gradient
    second_new = (
        second_decay * second.astype(jnp.float32) + (1.0 - second_decay) * gradient * gradient
    )
    step_dir = moment_new / first_bias / (jnp.sqrt(second_new / second_bias) + epsilon)
    weight_wide = weight.astype(jnp.float32)
    updated = weight_wide - learn_rate * (step_dir + weight_decay * weight_wide)
    return (
        updated.astype(jnp.bfloat16),
        moment_new.astype(jnp.bfloat16),
        second_new.astype(jnp.bfloat16),
    )


def per_device(
    attention_input,
    feedforward_input,
    attention_cotangent,
    feedforward_cotangent,
    lengths,
    groups,
    attention_weight,
    attention_moment,
    attention_second,
    feedforward_weight,
    feedforward_moment,
    feedforward_second,
):
    example_count = lengths.shape[0]
    attention_full, feedforward_full = rows_first((attention_input, feedforward_input), DP, (1, 1))
    slot_len = attention_full.shape[1] // example_count
    live_mask = live_tokens(lengths, slot_len)
    attention_live = jnp.where(live_mask[None, :], attention_full, jnp.zeros_like(attention_full))
    feedforward_live = jnp.where(
        live_mask[None, :], feedforward_full, jnp.zeros_like(feedforward_full)
    )
    attention_columns, feedforward_columns = side_by_side(
        (attention_cotangent, feedforward_cotangent), FSDP, 0, 1
    )
    attention_part = example_norms(attention_live, attention_columns, attention_second, slot_len)
    feedforward_part = example_norms(
        feedforward_live, feedforward_columns, feedforward_second, slot_len
    )
    norm_vals = by_axis(attention_part + feedforward_part, DP_FSDP)
    weights = importance(norm_vals, groups)
    token_weight = jnp.repeat(weights, slot_len) * live_mask.astype(jnp.float32)
    attention_grad = weighted_gradient(
        attention_live, attention_columns, token_weight, example_count
    )
    feedforward_grad = weighted_gradient(
        feedforward_live, feedforward_columns, token_weight, example_count
    )
    attention_new = adamw_step(attention_weight, attention_moment, attention_second, attention_grad)
    feedforward_new = adamw_step(
        feedforward_weight, feedforward_moment, feedforward_second, feedforward_grad
    )
    return (
        attention_new[0],
        attention_new[1],
        attention_new[2],
        feedforward_new[0],
        feedforward_new[1],
        feedforward_new[2],
    )


def solution(mesh):
    finer = Mesh(
        mesh.devices.reshape(4, 2, 4, 8, 4), ("dp_0", "dp_1", "fsdp_0", "fsdp_1", "fsdp_2")
    )
    in_specs = (
        P(FSDP, DP),
        P(FSDP, DP),
        P(DP_FSDP, None),
        P(DP_FSDP, None),
        P(),
        P(),
        P(FSDP, DP),
        P(FSDP, DP),
        P(FSDP, DP),
        P(FSDP, DP),
        P(FSDP, DP),
        P(FSDP, DP),
    )
    out_specs = (P(FSDP, DP), P(FSDP, DP), P(FSDP, DP), P(FSDP, DP), P(FSDP, DP), P(FSDP, DP))
    return jax.shard_map(
        per_device, mesh=finer, in_specs=in_specs, out_specs=out_specs, check_vma=False
    )
```

profile of v0, /device:TPU:1, one launch (start us, length us, event | category | flops | bytes accessed | tf_op | source)
XLA Modules:
  0.0 1220.1 jit_solution(11657597656473510270)
XLA Ops:
  10.4 54.4 %all-gather = bf16[8,192,176]{1,2,0:T(8,128)(2,1)S(1)} all-gather(bf16[1,192,176]{1,2,0:T(8,128)(2,1)S(1)} %maximum_bitcast_fusion), channel_id=1, replica_groups=mesh['dp_0'=4,'dp_1'=2,'fsdp_0'=4,'fsdp_1'=8,'fsdp_2'=4] {'dp_0','dp_1'}, dimensions={0}, use_global_device_ids=true | all-gather | bytes 608256 | tf_op jit(solution)/shard_map/all_gather | solution.py:25
  66.2 845.0 %all-gather.3.cloned.1.call-done = bf16[1024,3072]{1,0:T(8,128)(2,1)} async-done(((bf16[8,3072]{1,0:T(8,128)(2,1)}), bf16[1024,3072]{1,0:T(8,128)(2,1)}) %all-gather.3.cloned.1.call-update) | async-done | bytes 6291472 | tf_op jit(solution)/shard_map/all_gather | solution.py:36
  911.2 5.9 fusion.36
  917.2 64.1 %while.28 = (s32[]{:T(128)}, f32[24]{0:T(128)S(1)}, bf16[64,1536]{1,0:T(8,128)(2,1)S(1)}, bf16[1024,1536]{1,0:T(8,128)(2,1)}, f32[64,1024]{1,0:T(8,128)S(1)}, /*...) while((s32[]{:T(128)}, f32[24]{0:T(128)S(1)}, bf16[64,1536]{1,0:T(8,128)(2,1)S(1)}, ...), condition=%wide.region_3.4_spmd, body=%wide.region_1.0_spmd.sunk | while | flops 8585225 | bytes 542077 | solution.py:63
  917.2 1.9 fusion.45
  925.2 1.9 fusion.45
  927.9 1.9 fusion.45
  930.6 1.9 fusion.45
  943.9 1.9 fusion.45
  949.2 1.9 fusion.45
  951.9 1.9 fusion.45
  957.2 1.9 fusion.45
  965.2 1.9 fusion.45
  970.6 1.9 fusion.45
  973.2 1.9 fusion.45
  975.9 1.9 fusion.45
  981.2 65.2 %while.29 = (s32[]{:T(128)}, f32[24]{0:T(128)S(1)}, bf16[112,1536]{1,0:T(8,128)(2,1)S(1)}, bf16[1024,1536]{1,0:T(8,128)(2,1)}, f32[112,1024]{1,0:T(8,128)S(1)}, ...) while((s32[]{:T(128)}, f32[24]{0:T(128)S(1)}, bf16[112,1536]{1,0:T(8,128)(2,1)S(1)}, ...), condition=%wide.region_6.7_spmd, body=%wide.region_4.6_spmd.sunk | while | flops 15024137 | bytes 750973 | solution.py:63
  981.2 1.9 fusion.48
  984.0 1.9 fusion.48
  986.7 1.9 fusion.48
  989.4 1.9 fusion.48
  992.1 1.9 fusion.48
  994.8 1.9 fusion.48
  997.5 1.9 fusion.48
  1000.2 1.9 fusion.48
  1003.0 1.9 fusion.48
  1005.7 1.9 fusion.48
  1008.4 1.9 fusion.48
  1011.1 1.9 fusion.48
  1013.8 1.9 fusion.48
  1016.5 1.9 fusion.48
  1019.3 1.9 fusion.48
  1022.0 1.9 fusion.48
  1024.7 1.9 fusion.48
  1027.4 1.9 fusion.48
  1030.1 1.9 fusion.48
  1032.8 1.9 fusion.48
  1035.6 1.9 fusion.48
  1038.3 1.9 fusion.48
  1041.0 1.9 fusion.48
  1043.7 1.9 fusion.48
  1046.4 21.6 %psum.35 = f32[24]{0:T(128)S(1)} all-reduce(f32[24]{0:T(128)S(1)} %add.114), channel_id=1, replica_groups=mesh['dp_0'=4,'dp_1'=2,'fsdp_0'=4,'fsdp_1'=8,'fsdp_2'=4] {'dp_0'}, use_global_device_ids=true, to_apply=%region_7.8 | all-reduce | flops 24 | bytes 192 | tf_op jit(solution)/shard_map/psum | solution.py:42
  1068.0 99.2 %psum.36 = f32[24]{0:T(128)S(1)} all-reduce(f32[24]{0:T(128)S(1)} %psum.35), channel_id=1, replica_groups=mesh['dp_0'=4,'dp_1'=2,'fsdp_0'=4,'fsdp_1'=8,'fsdp_2'=4] {'dp_1'}, use_global_device_ids=true, to_apply=%region_8.9 | all-reduce | flops 24 | bytes 192 | tf_op jit(solution)/shard_map/psum | solution.py:42
  1167.3 6.1 psum.37
  1173.3 21.5 %psum.38 = f32[24]{0:T(128)S(1)} all-reduce(f32[24]{0:T(128)S(1)} %psum.37), channel_id=1, replica_groups=mesh['dp_0'=4,'dp_1'=2,'fsdp_0'=4,'fsdp_1'=8,'fsdp_2'=4] {'fsdp_1'}, use_global_device_ids=true, to_apply=%region_10.11 | all-reduce | flops 24 | bytes 192 | tf_op jit(solution)/shard_map/psum | solution.py:42
  1194.9 10.0 psum.39
  1205.3 3.8 fusion.31
  1209.1 4.1 fusion.26
  (98 shorter events, 66.1 us)
Async XLA Ops:
  7.2 58.5 %copy-start.3 = (s32[24]{0:T(128)S(1)}, s32[24]{0:T(128)}, u32[]{:S(2)}) copy-start(s32[24]{0:T(128)} %param.24) | copy-start | bytes 292
  7.2 58.7 %copy-start.1 = (bf16[64,1024]{1,0:T(8,128)(2,1)S(1)}, bf16[64,1024]{1,0:T(8,128)(2,1)}, u32[]{:S(2)}) copy-start(bf16[64,1024]{1,0:T(8,128)(2,1)} %param.28) | copy-start | bytes 393220
  7.2 58.8 %copy-start = (bf16[112,1024]{1,0:T(8,128)(2,1)S(1)}, bf16[112,1024]{1,0:T(8,128)(2,1)}, u32[]{:S(2)}) copy-start(bf16[112,1024]{1,0:T(8,128)(2,1)} %param.31) | copy-start | bytes 688132
  7.2 904.0 %all-gather.3.cloned.1.call-start = ((), (), s32[]{:S(2)}) async-start(), calls=%async_computation | async-start | bytes 6340608 | tf_op jit(solution)/shard_map/all_gather | solution.py:36
  917.1 287.8 %copy-start.2 = (s32[24]{0:T(128)S(1)}, s32[24]{0:T(128)}, u32[]{:S(2)}) copy-start(s32[24]{0:T(128)} %param.25) | copy-start | bytes 292
  917.1 288.1 %copy-start.6 = (bf16[64,1024]{1,0:T(8,128)(2,1)S(1)}, bf16[64,1024]{1,0:T(8,128)(2,1)}, u32[]{:S(2)}) copy-start(bf16[64,1024]{1,0:T(8,128)(2,1)} %param.27) | copy-start | bytes 393220
  917.1 288.1 %copy-start.7 = (bf16[64,1024]{1,0:T(8,128)(2,1)S(1)}, bf16[64,1024]{1,0:T(8,128)(2,1)}, u32[]{:S(2)}) copy-start(bf16[64,1024]{1,0:T(8,128)(2,1)} %param.26) | copy-start | bytes 393220
  1046.4 162.7 %copy-start.4 = (bf16[112,1024]{1,0:T(8,128)(2,1)S(1)}, bf16[112,1024]{1,0:T(8,128)(2,1)}, u32[]{:S(2)}) copy-start(bf16[112,1024]{1,0:T(8,128)(2,1)} %param.30) | copy-start | bytes 688132
  1046.4 162.7 %copy-start.5 = (bf16[112,1024]{1,0:T(8,128)(2,1)S(1)}, bf16[112,1024]{1,0:T(8,128)(2,1)}, u32[]{:S(2)}) copy-start(bf16[112,1024]{1,0:T(8,128)(2,1)} %param.29) | copy-start | bytes 688132
Sparse Core Ops, SparseCore 0:
  11.2 899.9 all-gather.2
where the time goes:
time: 1230 us; the launch traced here: 1220 us
  waiting for transfers between devices  845 us (69%)
  blocking collectives  213 us (17%)
  matrix products  98.1 us (8%)
  other arithmetic  41.9 us (3%)
  between operations  14.2 us (1%)
    all_gather x1, waiting for transfers between devices, side_by_side(): filled = lax.all_gather(both, axis, axis=dim, tiled=True)  845 us
    psum x5, blocking collectives, by_axis(): shard = lax.psum(shard, axis)  158 us
    dot_general x48, matrix products, one_example(): lax.dot_general(inputs_slot, grads_slot, (((1,), (1,)), ((), ())), prefer...  90.2 us
    all_gather x1, blocking collectives, rows_first(): filled, at, done = (lax.all_gather(both, axis, axis=0, tiled=True), 0, [])  54.4 us
    scatter x48, other arithmetic, one_example(): return norm_vals.at[example].set(jnp.sum(tile_block * tile_block * precond))  39 us
  transfers between devices with their start and end apart: 1, of which 1 were waited for; matrix products, arithmetic and copies ran while one was open for 0% of the time, Pallas kernels for 0%

commit v1 on v0

v1 whole, which is shorter than its diff:
```python
import functools

import jax
import jax.numpy as jnp
from jax import lax
from jax.experimental import pallas as pl
from jax.experimental.pallas import tpu as pltpu
from jax.sharding import Mesh
from jax.sharding import PartitionSpec as P

DP = ("dp_0", "dp_1")
FSDP = ("fsdp_0", "fsdp_1", "fsdp_2")
DP_FSDP = ("dp_0", "dp_1", "fsdp_0", "fsdp_1", "fsdp_2")


first_decay = 0.9
second_decay = 0.95
first_bias = 1.0 - 0.9**10
second_bias = 1.0 - 0.95**10
learn_rate = 0.01
weight_decay = 0.1
epsilon = 1e-08
norm_epsilon = 1e-06


def token_rows(arrays):
    both = jnp.concatenate(arrays, axis=0)
    filled = lax.all_gather(both, DP, axis=1, tiled=True)
    return filled


def column_rows(arrays):
    both = jnp.concatenate(arrays, axis=1)
    run = lax.all_gather(both, "fsdp_1", axis=0, tiled=False)
    plane = lax.all_gather(run, ("fsdp_0", "fsdp_2"), axis=0, tiled=False)
    plane = plane.reshape(4, 4, *run.shape)
    ordered = plane.transpose(0, 2, 1, 3, 4)
    return ordered.reshape(-1, both.shape[1])


def sum_everywhere(row):
    peers = lax.axis_size(FSDP)
    spread = jnp.broadcast_to(row[None, :], (peers, row.shape[0]))
    met = lax.all_to_all(spread, FSDP, 0, 0, tiled=True)
    part = jnp.sum(met, axis=0, keepdims=True)
    return jnp.sum(lax.all_gather(part, DP, axis=0, tiled=True), axis=0)


def live_tokens(lengths, slot_len):
    position = lax.broadcasted_iota(jnp.int32, (lengths.shape[0], slot_len), 1)
    return (position < lengths[:, None]).reshape(-1)


def norm_kernel(slot, lengths_ref, x_ref, ca_ref, cf_ref, va_ref, vf_ref, out_ref, pa_ref, pf_ref):
    step = pl.program_id(0)

    @pl.when(step == 0)
    def _():
        pa_ref[...] = 1.0 / (jnp.sqrt(va_ref[...].astype(jnp.float32)) + epsilon)
        pf_ref[...] = 1.0 / (jnp.sqrt(vf_ref[...].astype(jnp.float32)) + epsilon)
        out_ref[...] = jnp.zeros_like(out_ref)

    x = x_ref[...]
    rows_a, width = pa_ref.shape
    rows = x.shape[0]
    block = x.shape[1]
    per = block // slot
    position = lax.broadcasted_iota(jnp.int32, (rows, block), 1)
    chosen = []
    for j in range(per):
        live = lengths_ref[step * per + j]
        chosen.append(
            jnp.where((position >= j * slot) & (position < j * slot + live), x, jnp.zeros_like(x))
        )
    wide = 256
    for j in range(per):
        part = jnp.zeros((8, wide), jnp.float32)
        for at in range(0, width, wide):
            for c_ref, p_ref, low, high in (
                (ca_ref, pa_ref, 0, rows_a),
                (cf_ref, pf_ref, rows_a, rows),
            ):
                tile = lax.dot_general(
                    chosen[j][low:high],
                    c_ref[at : at + wide, :],
                    (((1,), (1,)), ((), ())),
                    preferred_element_type=jnp.float32,
                )
                share = tile * tile * p_ref[:, at : at + wide]
                part = part + jnp.sum(share.reshape(-1, 8, wide), axis=0)
        total = jnp.sum(part)
        row = lax.broadcasted_iota(jnp.int32, out_ref.shape, 1)
        out_ref[...] = out_ref[...] + jnp.where(row == step * per + j, total, 0.0)

def norms(x, columns, va, vf, lengths, slot, block=256):
    rows, tokens = x.shape
    width = columns.shape[0]
    steps = tokens // block
    return pl.pallas_call(
        functools.partial(norm_kernel, slot),
        out_shape=jax.ShapeDtypeStruct((8, 128), jnp.float32),
        grid=(steps,),
        in_specs=[
            pl.BlockSpec(memory_space=pltpu.SMEM),
            pl.BlockSpec((rows, block), lambda i: (0, i)),
            pl.BlockSpec((width, block), lambda i: (0, i)),
            pl.BlockSpec((width, block), lambda i, n=steps: (0, i + n)),
            pl.BlockSpec(va.shape, lambda i: (0, 0)),
            pl.BlockSpec(vf.shape, lambda i: (0, 0)),
        ],
        out_specs=pl.BlockSpec((8, 128), lambda i: (0, 0)),
        scratch_shapes=[pltpu.VMEM(va.shape, jnp.float32), pltpu.VMEM(vf.shape, jnp.float32)],
        compiler_params=pltpu.CompilerParams(dimension_semantics=("arbitrary",)),
        name="norms",
    )(lengths, x, columns, columns, va, vf)


def importance(norm_vals, groups):
    strength = jnp.sqrt(norm_vals + norm_epsilon)
    same_group = (groups[:, None] == groups[None, :]).astype(jnp.float32)
    group_total = jnp.sum(same_group * strength[None, :], axis=1)
    group_count = jnp.sum(same_group, axis=1)
    return group_count * strength / group_total


def weighted_gradient(inputs, cotangents, token_weight, example_count):
    scaled = (inputs.astype(jnp.float32) * token_weight[None, :]).astype(jnp.bfloat16)
    product = lax.dot_general(
        scaled, cotangents, (((1,), (1,)), ((), ())), preferred_element_type=jnp.float32
    )
    return product / example_count


def adamw_step(weight, moment, second, gradient):
    moment_new = first_decay * moment.astype(jnp.float32) + (1.0 - first_decay) * gradient
    second_new = (
        second_decay * second.astype(jnp.float32) + (1.0 - second_decay) * gradient * gradient
    )
    step_dir = moment_new / first_bias / (jnp.sqrt(second_new / second_bias) + epsilon)
    weight_wide = weight.astype(jnp.float32)
    updated = weight_wide - learn_rate * (step_dir + weight_decay * weight_wide)
    return (
        updated.astype(jnp.bfloat16),
        moment_new.astype(jnp.bfloat16),
        second_new.astype(jnp.bfloat16),
    )


def per_device(
    attention_input,
    feedforward_input,
    attention_cotangent,
    feedforward_cotangent,
    lengths,
    groups,
    attention_weight,
    attention_moment,
    attention_second,
    feedforward_weight,
    feedforward_moment,
    feedforward_second,
):
    example_count = lengths.shape[0]
    columns = column_rows((attention_cotangent, feedforward_cotangent))
    inputs = token_rows((attention_input, feedforward_input))
    tokens = inputs.shape[1]
    slot_len = tokens // example_count
    live_mask = live_tokens(lengths, slot_len)
    row = norms(inputs, columns, attention_second, feedforward_second, lengths, slot_len)
    norm_vals = sum_everywhere(row[0])[:example_count]
    weights = importance(norm_vals, groups)
    token_weight = jnp.repeat(weights, slot_len) * live_mask.astype(jnp.float32)
    attention_rows = attention_input.shape[0]
    live = jnp.where(live_mask[None, :], inputs, jnp.zeros_like(inputs))
    attention_grad = weighted_gradient(
        live[:attention_rows], columns[:, :tokens], token_weight, example_count
    )
    feedforward_grad = weighted_gradient(
        live[attention_rows:], columns[:, tokens:], token_weight, example_count
    )
    attention_new = adamw_step(attention_weight, attention_moment, attention_second, attention_grad)
    feedforward_new = adamw_step(
        feedforward_weight, feedforward_moment, feedforward_second, feedforward_grad
    )
    return (
        attention_new[0],
        attention_new[1],
        attention_new[2],
        feedforward_new[0],
        feedforward_new[1],
        feedforward_new[2],
    )


def solution(mesh):
    finer = Mesh(
        mesh.devices.reshape(4, 2, 4, 8, 4), ("dp_0", "dp_1", "fsdp_0", "fsdp_1", "fsdp_2")
    )
    in_specs = (
        P(FSDP, DP),
        P(FSDP, DP),
        P(DP_FSDP, None),
        P(DP_FSDP, None),
        P(),
        P(),
        P(FSDP, DP),
        P(FSDP, DP),
        P(FSDP, DP),
        P(FSDP, DP),
        P(FSDP, DP),
        P(FSDP, DP),
    )
    out_specs = (P(FSDP, DP), P(FSDP, DP), P(FSDP, DP), P(FSDP, DP), P(FSDP, DP), P(FSDP, DP))
    return jax.shard_map(
        per_device, mesh=finer, in_specs=in_specs, out_specs=out_specs, check_vma=False
    )
```

time: 1230 us -> 255 us (0.21)
  waiting for transfers between devices: 845 us -> 63.6 us
  matrix products: 98.1 us -> 7.94 us
  blocking collectives: 213 us -> 129 us
  other arithmetic: 41.9 us -> 1.92 us
  starting transfers between devices: 0.04 us -> 15.3 us
    all_gather x1, waiting for transfers between devices: 845 us -> 50.4 us  [column_rows(): plane = lax.all_gather(run, ('fsdp_0', 'fsdp_2'), axis=0, tiled=False)]
    psum x5 -> x0, blocking collectives: 158 us -> none  [by_axis(): shard = lax.psum(shard, axis)]
    dot_general x48 -> x0, matrix products: 90.2 us -> none  [one_example(): lax.dot_general(inputs_slot, grads_slot, (((1,), (1,)), ((), ())), prefer...]
    all_gather x1 -> x3, blocking collectives: 54.4 us -> 129 us  [the longest x1 53.9 us: token_rows(): filled = lax.all_gather(both, DP, axis=1, tiled=True)]
    scatter x48 -> x0, other arithmetic: 39 us -> none  [one_example(): return norm_vals.at[example].set(jnp.sum(tile_block * tile_block * precond))]
    all_to_all x0 -> x1, starting transfers between devices: none -> 15.2 us  [sum_everywhere(): met = lax.all_to_all(spread, FSDP, 0, 0, tiled=True)]
    all_to_all x0 -> x1, waiting for transfers between devices: none -> 13.2 us  [sum_everywhere(): met = lax.all_to_all(spread, FSDP, 0, 0, tiled=True)]
  transfers between devices with their start and end apart: 1 -> 2, of which waited for: 1 -> 2; matrix products, arithmetic and copies ran while one was open for 0% -> 1% of each run, Pallas kernels for 0% -> 0%
where the time goes in v1:
time: 255 us
  blocking collectives  129 us (51%)
  waiting for transfers between devices  63.6 us (25%)
  starting transfers between devices  15.3 us (6%)
  between operations  14.1 us (6%)
  Pallas kernels  12 us (5%)
  local copies, waits for them, and re-layouts  10.3 us (4%)
  matrix products  7.94 us (3%)
    all_gather x1, blocking collectives, token_rows(): filled = lax.all_gather(both, DP, axis=1, tiled=True)  53.9 us
    all_gather x1, waiting for transfers between devices, column_rows(): plane = lax.all_gather(run, ('fsdp_0', 'fsdp_2'), axis=0, tiled=False)  50.4 us
    all_gather x1, blocking collectives, column_rows(): run = lax.all_gather(both, 'fsdp_1', axis=0, tiled=False)  47.3 us
    all_gather x1, blocking collectives, sum_everywhere(): return jnp.sum(lax.all_gather(part, DP, axis=0, tiled=True), axis=0)  28.2 us
    all_to_all x1, starting transfers between devices, sum_everywhere(): met = lax.all_to_all(spread, FSDP, 0, 0, tiled=True)  15.2 us
    all_to_all x1, waiting for transfers between devices, sum_everywhere(): met = lax.all_to_all(spread, FSDP, 0, 0, tiled=True)  13.2 us
    pallas_call x1, Pallas kernels, norms(): pl.pallas_call(functools.partial(norm_kernel, slot), out_shape=jax.ShapeD...  12 us
    dot_general x2, matrix products, weighted_gradient(): lax.dot_general(scaled, cotangents, (((1,), (1,)), ((), ())), preferred_e...  7.94 us
  transfers between devices with their start and end apart: 2, of which 2 were waited for; matrix products, arithmetic and copies ran while one was open for 1% of the time, Pallas kernels for 0%

profile of v1, /device:TPU:1, one launch (start us, length us, event | category | flops | bytes accessed | tf_op | source)
XLA Modules:
  0.0 254.5 jit_solution(292795859225269923)
XLA Ops:
  7.2 0.0 all-gather.7.cloned.1.call-start
  7.2 0.8 pad_maximum_fusion
  8.0 47.3 %all-gather = bf16[64,3072]{1,0:T(8,128)(2,1)} all-gather(bf16[8,3072]{1,0:T(8,128)(2,1)S(1)} %pad_maximum_fusion), channel_id=2, replica_groups=mesh['dp_0'=4,'dp_1'=2,'fsdp_0'=4,'fsdp_1'=8,'fsdp_2'=4] {'fsdp_1'}, dimensions={0}, use_global_device_ids=true | all-gather | bytes 442368 | tf_op jit(solution)/shard_map/all_gather | solution.py:34
  55.3 0.0 all-gather.7.cloned.1.call-update
  55.3 0.9 copy.29
  56.2 0.8 maximum_bitcast_fusion
  57.0 53.9 %all-gather.3 = bf16[8,192,176]{1,2,0:T(8,128)(2,1)S(1)} all-gather(bf16[1,192,176]{1,2,0:T(8,128)(2,1)S(1)} %maximum_bitcast_fusion), channel_id=1, replica_groups=mesh['dp_0'=4,'dp_1'=2,'fsdp_0'=4,'fsdp_1'=8,'fsdp_2'=4] {'dp_0','dp_1'}, dimensions={0}, use_global_device_ids=true | all-gather | bytes 608256 | tf_op jit(solution)/shard_map/all_gather | solution.py:28
  110.9 0.2 copy.30
  111.1 1.4 reshape.67
  112.5 50.4 %all-gather.7.cloned.1.call-done = bf16[128,8,3072]{2,1,0:T(8,128)(2,1)} async-done(((bf16[8,8,3072]{2,1,0:T(8,128)(2,1)}), bf16[128,8,3072]{2,1,0:T(8,128)(2,1)}) %all-gather.7.cloned.1.call-update) | async-done | bytes 6291472 | tf_op jit(solution)/shard_map/all_gather | solution.py:35
  162.9 6.1 %copy.31 = bf16[4,8,4,8,3072]{4,3,2,1,0:T(8,128)(2,1)} copy(bf16[4,8,4,8,3072]{4,3,1,2,0:T(8,128)(2,1)} %bitcast.21) | data formatting | bytes 12582912 | tf_op jit(solution)/shard_map/transpose | solution.py:37
  169.0 0.0 copy-start.3
  169.0 0.0 copy-start
  169.0 0.0 copy-start.4
  169.0 0.0 copy-start.1
  169.0 0.0 copy-start.5
  169.0 0.0 copy-start.6
  169.0 12.0 %norms.1 = f32[8,128]{1,0:T(8,128)} custom-call(s32[24]{0:T(128)} %lengths_ref.1, bf16[176,1536]{1,0:T(8,128)(2,1)} %bitcast.22, bf16[1024,3072]{1,0:T(8,128)(2,1)} %bitcast.17, bf16[1024,3072]{1,0:T(8,128)(2,1)} %bitcast.18, bf16[64,1024]{1,0:T(8,128)(2,1)} %va_ref.1, bf16[112,1024]{1,0:T(8,128)(2,1)} %vf_ref.1), custom_call_target="tpu_custom_call" | custom-call | tf_op jit(solution)/shard_map/norms/pallas_call | solution.py:99
  181.0 0.0 copy-start.2
  181.0 0.0 copy-start.7
  181.0 0.0 copy-start.8
  181.0 0.7 slice_bitcast_fusion
  181.7 0.7 broadcast_in_dim.30
  182.4 15.2 %all-to-all-start = ((f32[128,1,128]{2,1,0:T(1,128)}), f32[128,1,128]{2,1,0:T(1,128)S(1)}, u32[]{:S(2)}, u32[]{:S(2)}) async-start(f32[128,1,128]{2,1,0:T(1,128)} %broadcast_in_dim.30), calls=%async_computation | async-start | bytes 131072 | tf_op jit(solution)/shard_map/all_to_all | solution.py:44
  197.6 0.0 copy-done.3
  197.7 0.1 iota_compare_fusion
  197.7 0.1 lt.21
  197.8 0.0 copy-done
  197.9 13.2 %all-to-all-done = f32[128,1,128]{2,1,0:T(1,128)S(1)} async-done(((f32[128,1,128]{2,1,0:T(1,128)}), f32[128,1,128]{2,1,0:T(1,128)S(1)}, u32[]{:S(2)}, u32[]{:S(2)}) %all-to-all-start) | async-done | bytes 65568 | tf_op jit(solution)/shard_map/all_to_all | solution.py:44
  211.1 28.2 %all-gather.4 = f32[8,1,128]{2,1,0:T(1,128)S(1)} all-gather(f32[1,1,128]{2,1,0:T(1,128)S(1)} %bitcast.25), channel_id=4, replica_groups=mesh['dp_0'=4,'dp_1'=2,'fsdp_0'=4,'fsdp_1'=8,'fsdp_2'=4] {'dp_0','dp_1'}, dimensions={0}, use_global_device_ids=true | all-gather | bytes 4608 | tf_op jit(solution)/shard_map/all_gather | solution.py:46
  239.4 0.0 copy-done.4
  239.4 0.2 fusion.18
  239.6 0.1 broadcast_in_dim.32
  239.6 0.1 reshape.61
  239.7 0.0 copy-done.1
  239.7 0.0 copy-done.5
  239.7 0.0 copy-done.6
  239.7 4.1 %fusion.13 = (bf16[112,1024]{1,0:T(8,128)(2,1)}, bf16[112,1024]{1,0:T(8,128)(2,1)}, bf16[112,1024]{1,0:T(8,128)(2,1)}) fusion(bf16[112,1024]{1,0:T(8,128)(2,1)S(1)} %copy-done.1, bf16[112,1024]{1,0:T(8,128)(2,1)S(1)} %copy-done.5, bf16[112,1024]{1,0:T(8,128)(2,1)S(1)} %copy-done.6, bf16[1024,3072]{1,0:T(8,128)(2,1)} %bitcast.19, ...), kind=kOutput, calls=%fused_computation.24 | convolution fusion | flops 355360768 | bytes 4874240 | tf_op jit(solution)/shard_map/dot_general | solution.py:128
  243.9 0.0 copy-done.2
  243.9 0.0 copy-done.7
  243.9 0.0 copy-done.8
  243.9 3.8 %fusion.17 = (bf16[64,1024]{1,0:T(8,128)(2,1)}, bf16[64,1024]{1,0:T(8,128)(2,1)}, bf16[64,1024]{1,0:T(8,128)(2,1)}) fusion(bf16[64,1024]{1,0:T(8,128)(2,1)S(1)} %copy-done.2, bf16[64,1024]{1,0:T(8,128)(2,1)S(1)} %copy-done.7, bf16[64,1024]{1,0:T(8,128)(2,1)S(1)} %copy-done.8, bf16[1024,3072]{1,0:T(8,128)(2,1)} %bitcast.20, ...), kind=kOutput, calls=%fused_computation.28 | convolution fusion | flops 203063296 | bytes 4136960 | tf_op jit(solution)/shard_map/dot_general | solution.py:128
  (6 shorter events, 0.1 us)
Async XLA Ops:
  7.2 155.7 %all-gather.7.cloned.1.call-start = ((), (), s32[]{:S(2)}) async-start(), calls=%async_computation.1 | async-start | bytes 6684672 | tf_op jit(solution)/shard_map/all_gather | solution.py:35
  169.0 28.7 %copy-start.3 = (s32[24]{0:T(128)S(1)}, s32[24]{0:T(128)}, u32[]{:S(2)}) copy-start(s32[24]{0:T(128)} %lengths_ref.1) | copy-start | bytes 292
  169.0 28.8 %copy-start = (bf16[1536,176]{0,1:T(8,128)(2,1)S(1)}, bf16[1536,176]{0,1:T(8,128)(2,1)}, u32[]{:S(2)}) copy-start(bf16[1536,176]{0,1:T(8,128)(2,1)} %reshape.67) | copy-start | bytes 1622020
  169.0 70.4 %copy-start.4 = (s32[24]{0:T(128)S(1)}, s32[24]{0:T(128)}, u32[]{:S(2)}) copy-start(s32[24]{0:T(128)} %param.17) | copy-start | bytes 292
  169.0 70.7 %copy-start.1 = (bf16[112,1024]{1,0:T(8,128)(2,1)S(1)}, bf16[112,1024]{1,0:T(8,128)(2,1)}, u32[]{:S(2)}) copy-start(bf16[112,1024]{1,0:T(8,128)(2,1)} %vf_ref.1) | copy-start | bytes 688132
  169.0 70.7 %copy-start.5 = (bf16[112,1024]{1,0:T(8,128)(2,1)S(1)}, bf16[112,1024]{1,0:T(8,128)(2,1)}, u32[]{:S(2)}) copy-start(bf16[112,1024]{1,0:T(8,128)(2,1)} %param.22) | copy-start | bytes 688132
  169.0 70.7 %copy-start.6 = (bf16[112,1024]{1,0:T(8,128)(2,1)S(1)}, bf16[112,1024]{1,0:T(8,128)(2,1)}, u32[]{:S(2)}) copy-start(bf16[112,1024]{1,0:T(8,128)(2,1)} %param.21) | copy-start | bytes 688132
  181.0 62.9 %copy-start.2 = (bf16[64,1024]{1,0:T(8,128)(2,1)S(1)}, bf16[64,1024]{1,0:T(8,128)(2,1)}, u32[]{:S(2)}) copy-start(bf16[64,1024]{1,0:T(8,128)(2,1)} %va_ref.1) | copy-start | bytes 393220
  181.0 62.9 %copy-start.7 = (bf16[64,1024]{1,0:T(8,128)(2,1)S(1)}, bf16[64,1024]{1,0:T(8,128)(2,1)}, u32[]{:S(2)}) copy-start(bf16[64,1024]{1,0:T(8,128)(2,1)} %param.19) | copy-start | bytes 393220
  181.0 62.9 %copy-start.8 = (bf16[64,1024]{1,0:T(8,128)(2,1)S(1)}, bf16[64,1024]{1,0:T(8,128)(2,1)}, u32[]{:S(2)}) copy-start(bf16[64,1024]{1,0:T(8,128)(2,1)} %param.18) | copy-start | bytes 393220
  182.4 28.7 %all-to-all-start = ((f32[128,1,128]{2,1,0:T(1,128)}), f32[128,1,128]{2,1,0:T(1,128)S(1)}, u32[]{:S(2)}, u32[]{:S(2)}) async-start(f32[128,1,128]{2,1,0:T(1,128)} %broadcast_in_dim.30), calls=%async_computation | async-start | bytes 131072 | tf_op jit(solution)/shard_map/all_to_all | solution.py:44
Sparse Core Ops, SparseCore 0:
  55.5 107.3 all-gather.6
